TPU v7x, 32 devices: a whole 2x2x4 slice. The times are simulated.
32 devices in a mesh: row: 4 (over y, x), col: 8 (over z, core).
Axes of the slice: x: 2, y: 2, z: 4, core: 2. Of those that a mesh axis runs over, the one named last changes fastest.
Arguments:
- pair_repr: bfloat16 [1024, 1024, 128], P('row', 'col'), may hold values from -6 to 6
- logit_cotangent: bfloat16 [1024, 1024, 128], P('row', 'col'), may hold values from -6 to 6
- pair_mask: int32 [1024, 1024], P('row', 'col'), may hold values 0 or 1
- single_repr: bfloat16 [1024, 384], P(('row', 'col')), may hold values from -6 to 6
- token_index: int32 [1024], replicated, may hold values from 0 to 2046, as said below
- pair_up: bfloat16 [128, 512], replicated, may hold values from -0.5 to 0.5
- pair_gate: bfloat16 [128, 512], replicated, may hold values from -0.5 to 0.5
- pair_down: bfloat16 [512, 128], replicated, may hold values from -0.25 to 0.25
- head_weight: bfloat16 [128, 128], replicated, may hold values from -0.5 to 0.5
- rel_table: bfloat16 [65, 128], replicated, may hold values from -3 to 3
- proj_row: bfloat16 [384, 128], replicated, may hold values from -0.3125 to 0.3125
- proj_col: bfloat16 [384, 128], replicated, may hold values from -0.3125 to 0.3125
- single_gate: bfloat16 [384, 1536], replicated, may hold values from -0.3125 to 0.3125
- single_up: bfloat16 [384, 1536], replicated, may hold values from -0.3125 to 0.3125
- single_down: bfloat16 [1536, 384], replicated, may hold values from -0.15625 to 0.15625
Outputs:
- pair_grad: bfloat16 [1024, 1024, 128], P('row', 'col')
- single_grad: bfloat16 [1024, 384], P(('row', 'col'))
- grad_pair_up: float32 [128, 512], replicated
- grad_pair_gate: float32 [128, 512], replicated
- grad_pair_down: float32 [512, 128], replicated
- grad_head: float32 [128, 128], replicated
- grad_rel: float32 [65, 128], replicated
- grad_proj_row: float32 [384, 128], replicated
- grad_proj_col: float32 [384, 128], replicated
- grad_single_gate: float32 [384, 1536], P(None, ('row', 'col'))
- grad_single_up: float32 [384, 1536], P(None, ('row', 'col'))
- grad_single_down: float32 [1536, 384], P(('row', 'col'))
Inputs may be any that keep to these rules, and one draw needn't show every extreme that they name: `token_index`: strictly increasing, entry 0 is 0, successive entries differ by 1 to 3, the last entry is 2046.
All inputs are finite; a program needn't handle non-finite values. No bound on the sum of `pair_mask` on one device may be relied on, other than what follows from the above.
Results may differ from a plain program's by a relative error of at most 0.018.
Values may be sent and summed in bfloat16 or wider, within the bound.
No kernel may reach another device: no remote copies, remote signals or barrier semaphores. Data moves between devices by JAX's collectives and lax.ppermute only.
A program may use at most 192 MiB of HBM per device.

v0:
```python
import functools

import jax
import jax.numpy as jnp
from jax import lax
from jax.experimental import pallas as pl
from jax.experimental.pallas import tpu as pltpu
from jax.sharding import PartitionSpec as P


norm_eps = 1e-05
lanes = 128
axes = ("row", "col")
f32 = jnp.float32
bf16 = jnp.bfloat16


def gated_parts(gate):
    sigma = jax.nn.sigmoid(gate)
    return (gate * sigma, sigma * (1.0 + gate * (1.0 - sigma)))


def product(matrix_a, matrix_b):
    return jnp.dot(matrix_a, matrix_b, preferred_element_type=f32)


def product_left(matrix_a, matrix_b):
    return lax.dot_general(matrix_a, matrix_b, (((0,), (0,)), ((), ())), preferred_element_type=f32)


def product_right(matrix_a, matrix_b):
    return lax.dot_general(matrix_a, matrix_b, (((1,), (1,)), ((), ())), preferred_element_type=f32)


def prepare_kernel(n_parts, idx_ref, cot_ref, mask_ref, *refs):
    outs, turned_ref = refs[:-1], refs[-1]
    _, _, n_rows, n_cols, width = cot_ref.shape
    bins = width // 2
    low_t = mask_ref[0, 0].astype(f32).T
    high_t = mask_ref[0, 1].astype(f32).T
    lane = lax.broadcasted_iota(jnp.int32, (n_cols, width), 1)
    for i in range(n_rows):
        low = pltpu.roll(cot_ref[0, 0, i].astype(f32), bins, 1) * low_t[:, i:i + 1]
        high = cot_ref[0, 1, i].astype(f32) * high_t[:, i:i + 1]
        turned_ref[:, i, :] = jnp.where(lane < bins, low, high)
    n_cols_piece = n_cols // n_parts
    for turn in range(len(outs) // n_parts):
        @pl.when(pl.program_id(0) == turn)
        def _(turn=turn):
            for part in range(n_parts):
                outs[turn * n_parts + part][...] = turned_ref[
                    part * n_cols_piece:(part + 1) * n_cols_piece
                ].astype(bf16)


def gates(both):
    hidden = both.shape[1] // 2
    up_pre, gate_pre = both[:, :hidden], both[:, hidden:]
    sigma = jnp.tanh(gate_pre * 0.5) * 0.5 + 0.5
    silu = gate_pre * sigma
    return up_pre, sigma, silu, silu * up_pre


def forward_kernel(
    span, n_given, pair_ref, row_ref, col_ref, rpos_ref, cpos_ref, table_ref, up_gate_ref, down_ref, *refs
):
    both_ref, norm_ref, norm_t_ref, inv_ref, out_t_ref = refs[n_given:]
    n_cols, width = pair_ref.shape[1:]
    n_rows = min(pair_ref.shape[0], 1024 // n_cols)
    count = n_rows * n_cols
    for sub in range(pair_ref.shape[0] // n_rows):
        rows = slice(sub * n_rows, (sub + 1) * n_rows)
        flat = slice(sub * count, (sub + 1) * count)
        offset = jnp.clip(rpos_ref[rows][:, None, :] - cpos_ref[...][None, :, :], -span, span) + span
        lane = lax.broadcasted_iota(jnp.int32, offset.shape, 2)
        hot = jnp.where(offset == lane, 1.0, 0.0).astype(bf16).reshape(count, lanes)
        pair_in = pair_ref[rows].astype(f32) + row_ref[rows][:, None, :] + col_ref[...][None, :, :]
        pair_in = pair_in.reshape(count, width) + product(hot, table_ref[...])
        centred = pair_in - jnp.mean(pair_in, axis=-1, keepdims=True)
        inv_std = lax.rsqrt(jnp.mean(centred * centred, axis=-1, keepdims=True) + norm_eps)
        normed_bf = (centred * inv_std).astype(bf16)
        norm_ref[flat] = normed_bf
        norm_t_ref[0, :, flat] = normed_bf.T
        inv_ref[flat] = jnp.broadcast_to(inv_std, (count, width)).astype(bf16)
        both = product(normed_bf, up_gate_ref[...]).astype(bf16)
        both_ref[flat] = both
        hid = gates(both)[3]
        pair_out = (pair_in + product(hid, down_ref[...])).astype(bf16)
        out_t_ref[0, :, flat] = pair_out.T


def backward_kernel(n_pieces, n_given, idx_ref, cot_ref, mask_ref, *refs):
    mirror_refs = refs[:n_pieces]
    (both_ref, norm_ref, norm_t_ref, inv_ref, out_t_ref, bucket_ref,
     head_t_ref, down_t_ref, up_t_ref, gate_t_ref) = refs[n_pieces:n_pieces + 10]
    refs = refs[n_pieces + 10 + n_given:]
    grad_ref, rows_ref, cols_ref, sums_ref, mir_ref, ug_acc, down_acc, head_acc, rel_acc = refs
    piece = pl.program_id(0)
    step = pl.program_id(1)
    first = (piece == 0) & (step == 0)
    last = (piece == pl.num_programs(0) - 1) & (step == pl.num_programs(1) - 1)
    n_cols, width = cot_ref.shape[1:]
    n_rows = min(cot_ref.shape[0], 1024 // n_cols)
    count = n_rows * n_cols
    half = n_cols // 2
    hidden = down_t_ref.shape[1]
    bins = width // 2

    @pl.when(first)
    def _():
        cols_ref[...] = jnp.zeros_like(cols_ref)
        ug_acc[...] = jnp.zeros_like(ug_acc)
        down_acc[...] = jnp.zeros_like(down_acc)
        head_acc[...] = jnp.zeros_like(head_acc)
        rel_acc[...] = jnp.zeros_like(rel_acc)

    for t in range(n_pieces):
        @pl.when(piece == t)
        def _(t=t):
            mir_ref[...] = mirror_refs[t][...]

    for sub in range(cot_ref.shape[0] // n_rows):
        rows = slice(sub * n_rows, (sub + 1) * n_rows)
        flat = slice(sub * count, (sub + 1) * count)
        packed = mir_ref[rows].astype(f32).reshape(n_rows * half, width)
        turned = pltpu.roll(packed, bins, 1).reshape(n_rows, half, width)
        mirrored = jnp.concatenate([turned, packed.reshape(n_rows, half, width)], axis=1)
        lane = lax.broadcasted_iota(jnp.int32, mirrored.shape, 2)
        mask_t = mask_ref[rows].astype(f32).T
        own = jnp.stack([cot_ref[sub * n_rows + i].astype(f32) * mask_t[:, i:i + 1] for i in range(n_rows)], axis=0)
        head_cot = (own + jnp.where(lane >= bins, mirrored, 0.0)).astype(bf16).reshape(count, width)
        grad_out = product(head_cot, head_t_ref[...])
        grad_out_bf = grad_out.astype(bf16)
        grad_hid = product(grad_out_bf, down_t_ref[...]).astype(bf16)
        up_pre, sigma, silu, hid = gates(both_ref[flat])
        grad_up = grad_hid * silu
        grad_gate = grad_hid * (up_pre * (sigma + silu * (1.0 - sigma)))
        grad_normed = product(grad_up, up_t_ref[...]) + product(grad_gate, gate_t_ref[...])
        normed = norm_ref[flat].astype(f32)
        grad_in = grad_out + inv_ref[flat].astype(f32) * (
            grad_normed
            - jnp.mean(grad_normed, axis=-1, keepdims=True)
            - normed * jnp.mean(grad_normed * normed, axis=-1, keepdims=True)
        )
        grad_tile = grad_in.reshape(n_rows, n_cols, width)
        grad_bf = grad_in.astype(bf16)
        grad_ref[rows] = grad_bf.reshape(n_rows, n_cols, width)
        rows_ref[rows] = jnp.sum(grad_tile, axis=1)
        cols_ref[...] += jnp.sum(grad_tile, axis=0)
        norm_t = norm_t_ref[0, :, flat]
        ug_acc[:, :hidden] += product(norm_t, grad_up)
        ug_acc[:, hidden:] += product(norm_t, grad_gate)
        down_acc[...] += product(grad_out_bf.T, hid)
        head_acc[...] += product(out_t_ref[0, :, flat], head_cot)
        level = lax.broadcasted_iota(jnp.int32, (lanes, count), 0)
        bucket = jnp.broadcast_to(bucket_ref[0, :, flat], (lanes, count))
        rel_acc[...] += product(jnp.where(bucket == level, 1.0, 0.0).astype(bf16), grad_bf)

    @pl.when(last)
    def _():
        n_slabs = hidden // lanes
        for q in range(2 * n_slabs):
            sums_ref[q] = ug_acc[:, q * lanes:(q + 1) * lanes]
        for q in range(n_slabs):
            sums_ref[2 * n_slabs + q] = down_acc[:, q * lanes:(q + 1) * lanes].T
        sums_ref[3 * n_slabs] = head_acc[...]
        sums_ref[3 * n_slabs + 1] = rel_acc[...]


def transition(tokens_in, single_gate, single_up, single_down):
    src = tokens_in.astype(f32)
    inv_rms = lax.rsqrt(jnp.mean(src * src, axis=-1, keepdims=True) + norm_eps)
    normed_bf = (src * inv_rms).astype(bf16)
    silu, _ = gated_parts(product(normed_bf, single_gate))
    hid = (silu * product(normed_bf, single_up)).astype(bf16)
    updated = (src + product(hid, single_down)).astype(bf16)
    return normed_bf, hid, updated


def gather_all(piece, n_dev):
    copies = jnp.broadcast_to(piece[None], (n_dev,) + piece.shape)
    return lax.all_to_all(copies, axes, split_axis=0, concat_axis=0, tiled=True)


def local(
    pair_repr, logit_cotangent, pair_mask, single_repr, token_index, pair_up, pair_gate, pair_down, head_weight,
    rel_table, proj_row, proj_col, single_gate, single_up, single_down,
):
    n_row = lax.axis_size("row")
    n_col = lax.axis_size("col")
    n_dev = n_row * n_col
    fold = n_col // n_row
    row_index = lax.axis_index("row")
    col_index = lax.axis_index("col")
    joint_index = row_index * n_col + col_index
    core = col_index % fold
    tile_rows, tile_cols, width = pair_repr.shape
    half = tile_cols // 2
    strip = single_repr.shape[0]
    tokens = strip * n_dev
    hidden = pair_up.shape[1]
    s_hidden = single_gate.shape[1]
    share = s_hidden // n_dev
    n_rel = rel_table.shape[0]
    span = (n_rel - 1) // 2
    n_groups = 2 if n_row % 2 == 0 else 1
    per_turn = n_row // fold
    piece_rows = tile_cols // per_turn
    block_rows = min(2048 // tile_cols, piece_rows)
    count = block_rows * tile_cols
    n_blocks = tile_rows // block_rows
    n_slabs = hidden // lanes
    n_sums = 3 * n_slabs + 2

    core_arr = core.astype(jnp.int32).reshape(1)
    n_parts = per_turn
    group = 16
    blocks = half // group

    def part_map(s, i, idx):
        return ((idx[0] + s) % fold, 0, i, 0, 0)

    def sent_map(s, i, idx, own=0):
        return (0, jnp.where(s == own, i, jnp.where(s < own, 0, blocks - 1)), 0)

    parted = (fold, 2, half, tile_cols)
    prepared = pl.pallas_call(
        functools.partial(prepare_kernel, n_parts),
        grid_spec=pltpu.PrefetchScalarGridSpec(
            num_scalar_prefetch=1,
            grid=(fold, blocks),
            in_specs=[
                pl.BlockSpec((1, 2, group, tile_cols, width), part_map),
                pl.BlockSpec((1, 2, group, tile_cols), lambda s, i, idx: part_map(s, i, idx)[:4]),
            ],
            out_specs=[
                pl.BlockSpec((piece_rows, group, width), functools.partial(sent_map, own=t // n_parts))
                for t in range(fold * n_parts)
            ],
            scratch_shapes=[pltpu.VMEM((tile_cols, group, width), f32)],
        ),
        out_shape=[jax.ShapeDtypeStruct((piece_rows, half, width), bf16)] * (fold * n_parts),
        cost_estimate=pl.CostEstimate(
            flops=tile_rows * tile_cols * width * 4, bytes_accessed=tile_rows * tile_cols * width * 3, transcendentals=0
        ),
        name="mask_and_turn",
    )(core_arr, logit_cotangent.reshape(parted + (width,)), pair_mask.reshape(parted))
    sent = prepared

    def place(r, k, b):
        return r * n_col + k * fold + b

    every = [(r, k, b) for r in range(n_row) for k in range(n_row) for b in range(fold)]

    def onward(t):
        s = t // per_turn
        return [(place((r + k + t) % n_row, k, b), place(k, r, (b + s) % fold)) for r, k, b in every]

    order = [t for group_no in range(n_groups) for t in range(group_no, n_row, n_groups)]
    pieces = {}
    for t in order:
        spread = [(place(r, k, b), place((r + k + t) % n_row, k, b)) for r, k, b in every]
        pieces[t] = lax.ppermute(sent[t], axes, spread)
    singles = gather_all(single_repr, n_dev).reshape(tokens, -1)

    row_pos = lax.dynamic_slice_in_dim(token_index, row_index * tile_rows, tile_rows, 0)
    col_pos = lax.dynamic_slice_in_dim(token_index, col_index * tile_cols, tile_cols, 0)
    rpos = jnp.broadcast_to(row_pos[:, None], (tile_rows, lanes))
    cpos = jnp.broadcast_to(col_pos[:, None], (tile_cols, lanes))
    bucket = (jnp.clip(row_pos[:, None] - col_pos[None, :], -span, span) + span).reshape(n_blocks, 1, count)
    table = jnp.pad(rel_table, ((0, lanes - n_rel), (0, 0)))
    up_gate = jnp.concatenate([pair_up, pair_gate], axis=1)

    singles, rpos, cpos, bucket, table, up_gate = lax.optimization_barrier(
        (singles, rpos, cpos, bucket, table, up_gate)
    )
    near = jnp.concatenate(
        [
            lax.dynamic_slice_in_dim(singles, row_index * tile_rows, tile_rows, 0),
            lax.dynamic_slice_in_dim(singles, col_index * tile_cols, tile_cols, 0),
        ],
        axis=0,
    )
    near_updated = transition(near, single_gate, single_up, single_down)[2]
    row_proj = product(near_updated[:tile_rows], proj_row).astype(bf16).astype(f32)
    col_proj = product(near_updated[tile_rows:], proj_col).astype(bf16).astype(f32)

    n_pairs = tile_rows * tile_cols
    whole = lambda shape: pl.BlockSpec(shape, lambda *_: (0,) * len(shape))
    flat = lambda cols_, where: pl.BlockSpec((count, cols_), lambda *at: (where(*at), 0))
    lead = lambda shape, where: pl.BlockSpec((1,) + shape, lambda *at: (where(*at), 0, 0))
    tile = lambda where: pl.BlockSpec((block_rows, tile_cols, width), lambda *at: (where(*at), 0, 0))
    some = lambda cols_, where: pl.BlockSpec((block_rows, cols_), lambda *at: (where(*at), 0))
    saved = ()
    n_early = n_blocks * 3 // 8
    for low, high in ((0, n_early), (n_early, n_blocks)):
        part = lambda i, low=low: i + low
        operands = [pair_repr, row_proj, col_proj, rpos, cpos, table, up_gate, pair_down]
        saved = pl.pallas_call(
            functools.partial(forward_kernel, span, len(saved)),
            grid=(high - low,),
            in_specs=[
                tile(part), some(width, part), whole((tile_cols, width)), some(lanes, part), whole((tile_cols, lanes)),
                whole(table.shape), whole(up_gate.shape), whole(pair_down.shape),
            ]
            + [pl.BlockSpec(memory_space=pl.ANY)] * len(saved),
            out_specs=[
                flat(2 * hidden, part), flat(width, part), lead((width, count), part), flat(width, part),
                lead((width, count), part),
            ],
            out_shape=[
                jax.ShapeDtypeStruct((n_pairs, 2 * hidden), bf16),
                jax.ShapeDtypeStruct((n_pairs, width), bf16),
                jax.ShapeDtypeStruct((n_blocks, width, count), bf16),
                jax.ShapeDtypeStruct((n_pairs, width), bf16),
                jax.ShapeDtypeStruct((n_blocks, width, count), bf16),
            ],
            input_output_aliases={len(operands) + i: i for i in range(len(saved))},
            cost_estimate=pl.CostEstimate(
                flops=2 * n_pairs * width * (3 * hidden + lanes) * (high - low) // n_blocks,
                bytes_accessed=n_pairs * (4 * hidden + 10 * width) * (high - low) // n_blocks,
                transcendentals=n_pairs * hidden * (high - low) // n_blocks,
            ),
            name="pair_forward",
        )(*operands, *saved)
        if low == 0:
            held, inv_held = lax.optimization_barrier((pieces, saved[3]))
            saved = list(saved[:3]) + [inv_held] + list(saved[4:])
            for t in range(0, n_row, n_groups):
                pieces[t] = lax.ppermute(held[t], axes, onward(t))
    late = [t for t in range(n_row) if t % n_groups]
    if late:
        held, inv_held = lax.optimization_barrier((held, saved[3]))
        saved = list(saved[:3]) + [inv_held] + list(saved[4:])
        for t in late:
            pieces[t] = lax.ppermute(held[t], axes, onward(t))

    head_t = head_weight.T
    down_t = pair_down.T
    up_t = pair_up.T
    gate_t = pair_gate.T
    steps = piece_rows // block_rows
    n_pieces = n_row // n_groups
    given = ()
    sums, cols = 0.0, 0.0
    for group_no in range(n_groups):
        def block_of(p, j, idx, group_no=group_no):
            t = p * n_groups + group_no
            strip_no = (idx[0] + fold - t // per_turn) % fold
            return strip_no * (tile_cols // block_rows) + (t % per_turn) * steps + j

        def mirror_map(p, j, idx, own=0):
            return (jnp.where(p == own, j, jnp.where(p < own, 0, steps - 1)), 0, 0)

        in_specs = (
            [tile(block_of), some(tile_cols, block_of)]
            + [
                pl.BlockSpec((block_rows, half, width), functools.partial(mirror_map, own=p))
                for p in range(n_pieces)
            ]
            + [flat(2 * hidden, block_of), flat(width, block_of), lead((width, count), block_of),
               flat(width, block_of), lead((width, count), block_of), lead((1, count), block_of),
               whole(head_t.shape), whole(down_t.shape), whole(up_t.shape), whole(gate_t.shape)]
            + [pl.BlockSpec(memory_space=pl.ANY)] * len(given)
        )
        operands = [logit_cotangent, pair_mask] + [pieces[p * n_groups + group_no] for p in range(n_pieces)] + list(saved) + [
            bucket, head_t, down_t, up_t, gate_t] + list(given)
        first_given = 1 + len(operands) - len(given)
        pair_grad, row_part, col_part, sum_part = pl.pallas_call(
            functools.partial(backward_kernel, n_pieces, len(given)),
            grid_spec=pltpu.PrefetchScalarGridSpec(
                num_scalar_prefetch=1,
                grid=(n_pieces, steps),
                in_specs=in_specs,
                out_specs=[
                    tile(block_of), some(width, block_of), whole((tile_cols, width)), whole((n_sums, lanes, lanes)),
                ],
                scratch_shapes=[
                    pltpu.VMEM((block_rows, half, width), bf16),
                    pltpu.VMEM((width, 2 * hidden), f32),
                    pltpu.VMEM((width, hidden), f32),
                    pltpu.VMEM((width, lanes), f32),
                    pltpu.VMEM((lanes, width), f32),
                ],
            ),
            out_shape=[
                jax.ShapeDtypeStruct(pair_repr.shape, bf16),
                jax.ShapeDtypeStruct((tile_rows, width), f32),
                jax.ShapeDtypeStruct((tile_cols, width), f32),
                jax.ShapeDtypeStruct((n_sums, lanes, lanes), f32),
            ],
            input_output_aliases={first_given + i: i for i in range(len(given))},
            cost_estimate=pl.CostEstimate(
                flops=2 * n_pairs * width * (6 * hidden + 3 * lanes) // n_groups,
                bytes_accessed=n_pairs * (4 * hidden + 13 * width) // n_groups,
                transcendentals=n_pairs * hidden // n_groups,
            ),
            name="pair_backward",
        )(core_arr, *operands)
        given = (pair_grad, row_part)
        sums = sums + sum_part
        cols = cols + col_part

    sum_rows = n_sums * lanes // n_dev

    def spread_out(part):
        size = part.size // n_dev
        narrow = min(size, lanes)
        return jnp.pad(part.reshape(n_dev, size // narrow, narrow), ((0, 0), (0, 0), (0, lanes - narrow)))

    row_sent, col_sent = spread_out(row_part), spread_out(cols)
    row_len, col_len = row_sent.shape[1], col_sent.shape[1]
    outgoing = jnp.concatenate([sums.reshape(n_dev, sum_rows, lanes), row_sent, col_sent], axis=1).astype(bf16)
    outgoing, singles = lax.optimization_barrier((outgoing, singles))
    s_normed_bf, _, updated = transition(singles, single_gate, single_up, single_down)
    arrived = lax.all_to_all(outgoing, axes, split_axis=0, concat_axis=0, tiled=True).astype(f32)
    row_own = jnp.sum(arrived[:, sum_rows:sum_rows + row_len].reshape(n_row, n_col, row_len, lanes), axis=1)
    col_own = jnp.sum(arrived[:, sum_rows + row_len:].reshape(n_row, n_col, col_len, lanes), axis=0)
    totals = jnp.concatenate(
        [row_own.reshape(n_row * row_len, lanes), col_own.reshape(n_col * col_len, lanes)], axis=0
    ).astype(bf16)
    grad_scale = 1.0 / tokens
    own_sums = (jnp.sum(arrived[:, :sum_rows], axis=0) * grad_scale).astype(bf16)
    totals_all = gather_all(totals, n_dev)
    own_sums, totals_all = lax.optimization_barrier((own_sums, totals_all))
    shared = gather_all(own_sums, n_dev)
    slabs = shared.reshape(n_sums, lanes, lanes).astype(f32)

    def tokens_of(held, n_strips, length):
        used = tokens * width // (n_strips * n_dev * length)
        return held.reshape(n_dev, n_strips, length, lanes)[..., :used].transpose(1, 0, 2, 3).reshape(tokens, width)

    row_bf = tokens_of(totals_all[:, :n_row * row_len], n_row, row_len)
    col_bf = tokens_of(totals_all[:, n_row * row_len:], n_col, col_len)

    single_cot = product_right(row_bf, proj_row) + product_right(col_bf, proj_col)
    cot_bf = single_cot.astype(bf16)
    prow_sum = product_left(updated, row_bf)
    pcol_sum = product_left(updated, col_bf)
    gate_cols = lax.dynamic_slice_in_dim(single_gate, joint_index * share, share, 1)
    up_cols = lax.dynamic_slice_in_dim(single_up, joint_index * share, share, 1)
    down_rows = lax.dynamic_slice_in_dim(single_down, joint_index * share, share, 0)
    own_up = product(s_normed_bf, up_cols)
    own_silu, own_slope = gated_parts(product(s_normed_bf, gate_cols))
    own_hid = (own_silu * own_up).astype(bf16)
    own_grad_hid = product_right(cot_bf, down_rows)
    own_grad_up = (own_grad_hid * own_silu).astype(bf16)
    own_grad_gate = (own_grad_hid * own_up * own_slope).astype(bf16)
    gate_sum = product_left(s_normed_bf, own_grad_gate)
    up_sum = product_left(s_normed_bf, own_grad_up)
    down_sum = product_left(own_hid, cot_bf)

    mine = lambda whole_: lax.dynamic_slice_in_dim(whole_, joint_index * strip, strip, 0)
    my_src = single_repr.astype(f32)
    my_inv = lax.rsqrt(jnp.mean(my_src * my_src, axis=-1, keepdims=True) + norm_eps)
    my_normed = my_src * my_inv
    my_normed_bf = my_normed.astype(bf16)
    my_up = product(my_normed_bf, single_up)
    my_silu, my_slope = gated_parts(product(my_normed_bf, single_gate))
    my_cot = mine(single_cot)
    my_grad_hid = product_right(my_cot.astype(bf16), single_down)
    my_grad_up = (my_grad_hid * my_silu).astype(bf16)
    my_grad_gate = (my_grad_hid * my_up * my_slope).astype(bf16)
    my_grad_normed = product_right(my_grad_gate, single_gate) + product_right(my_grad_up, single_up)
    single_grad = my_cot + my_inv * (
        my_grad_normed - my_normed * jnp.mean(my_grad_normed * my_normed, axis=-1, keepdims=True)
    )

    def wide(first):
        return slabs[first:first + n_slabs].transpose(1, 0, 2).reshape(width, hidden)

    return (
        pair_grad,
        single_grad.astype(bf16),
        wide(0),
        wide(n_slabs),
        slabs[2 * n_slabs:3 * n_slabs].reshape(hidden, width),
        slabs[3 * n_slabs],
        slabs[3 * n_slabs + 1][:n_rel],
        prow_sum * grad_scale,
        pcol_sum * grad_scale,
        gate_sum * grad_scale,
        up_sum * grad_scale,
        down_sum * grad_scale,
    )


def solution(mesh):
    placed = (
        P("row", "col", None),
        P("row", "col", None),
        P("row", "col"),
        P(("row", "col"), None),
    ) + (P(),) * 11
    return jax.shard_map(
        local,
        mesh=mesh,
        in_specs=placed,
        out_specs=(P("row", "col", None), P(("row", "col"), None))
        + (P(),) * 7
        + (P(None, ("row", "col")), P(None, ("row", "col")), P(("row", "col"), None)),
        check_vma=False,
    )
```

profile of v0, /device:TPU:0, one launch (start us, length us, event | category | flops | bytes accessed | tf_op | source)
XLA Modules:
  0.0 336.9 jit_solution(372827532378106025)
XLA Ops:
  0.7 1.8 broadcast_in_dim.16
  2.4 7.3 %all-to-all-start = ((bf16[32,32,384]{2,1,0:T(8,128)(2,1)}), bf16[32,32,384]{2,1,0:T(8,128)(2,1)S(1)}, u32[]{:S(2)}, u32[]{:S(2)}) async-start(bf16[32,32,384]{2,1,0:T(8,128)(2,1)} %broadcast_in_dim.16), calls=%async_computation | async-start | bytes 1572864 | tf_op jit(solution)/shard_map/all_to_all | solution.py:182
  9.8 12.2 %mask_and_turn.1 = (bf16[64,64,128]{2,1,0:T(8,128)(2,1)}, bf16[64,64,128]{2,1,0:T(8,128)(2,1)}, bf16[64,64,128]{2,1,0:T(8,128)(2,1)}, bf16[64,64,128]{2,1,0:T(8,128)(2,1)}) custom-call(s32[1]{0:T(128)} %bitcast.idx_ref, bf16[2,2,64,128,128]{4,3,2,1,0:T(8,128)(2,1)} %bitcast.65, s32[2,2,64,128]{3,2,1,0:T(8,128)} %bitcast.80), custom_call_target="tpu_custom_call" | custom-call | flops 16777216 | bytes 12582912 | tf_op jit(solution)/shard_map/mask_and_turn/pallas_call | solution.py:227
  22.0 9.5 %collective-permute-start = (bf16[64,64,128]{2,1,0:T(8,128)(2,1)}, bf16[64,64,128]{2,1,0:T(8,128)(2,1)}, u32[]{:S(2)}, u32[]{:S(2)}) collective-permute-start(bf16[64,64,128]{2,1,0:T(8,128)(2,1)} %get-tuple-element.52), channel_id=1, source_target_pairs={{0,0},{1,1},{2,10},{3,11},{4,20},{5,21},{6,30},{7,31},{8,8},{9,9},... | collective-permute-start | bytes 3145736 | tf_op jit(solution)/shard_map/ppermute | solution.py:263
  31.5 3.7 %collective-permute-start.1 = (bf16[64,64,128]{2,1,0:T(8,128)(2,1)}, bf16[64,64,128]{2,1,0:T(8,128)(2,1)}, u32[]{:S(2)}, u32[]{:S(2)}) collective-permute-start(bf16[64,64,128]{2,1,0:T(8,128)(2,1)} %get-tuple-element.53), channel_id=1, source_target_pairs={{0,8},{1,9},{2,18},{3,19},{4,28},{5,29},{6,6},{7,7},{8,16},{9,17},... | collective-permute-start | bytes 3145736 | tf_op jit(solution)/shard_map/ppermute | solution.py:263
  35.2 3.4 %collective-permute-start.2 = (bf16[64,64,128]{2,1,0:T(8,128)(2,1)}, bf16[64,64,128]{2,1,0:T(8,128)(2,1)}, u32[]{:S(2)}, u32[]{:S(2)}) collective-permute-start(bf16[64,64,128]{2,1,0:T(8,128)(2,1)} %get-tuple-element.54), channel_id=1, source_target_pairs={{0,16},{1,17},{2,26},{3,27},{4,4},{5,5},{6,14},{7,15},{8,24},{9,25... | collective-permute-start | bytes 3145736 | tf_op jit(solution)/shard_map/ppermute | solution.py:263
  38.6 3.4 %collective-permute-start.3 = (bf16[64,64,128]{2,1,0:T(8,128)(2,1)}, bf16[64,64,128]{2,1,0:T(8,128)(2,1)}, u32[]{:S(2)}, u32[]{:S(2)}) collective-permute-start(bf16[64,64,128]{2,1,0:T(8,128)(2,1)} %get-tuple-element.55), channel_id=1, source_target_pairs={{0,24},{1,25},{2,2},{3,3},{4,12},{5,13},{6,22},{7,23},{8,0},{9,1},... | collective-permute-start | bytes 3145736 | tf_op jit(solution)/shard_map/ppermute | solution.py:263
  47.6 2.2 fusion.16
  49.8 4.2 %fusion.7 = bf16[384,384]{1,0:T(8,128)(2,1)} fusion(bf16[1536,384]{1,0:T(8,128)(2,1)} %param.29, bf16[384,1536]{1,0:T(8,128)(2,1)S(1)} %copy-done.1, f32[384,1536]{1,0:T(8,128)} %fusion.16, f32[384]{0:T(512)S(1)} %add_rsqrt_fusion.1, bf16[128,384]{1,0:T(8,128)(2,1)S(1)} %constant_dynamic-slice_fusion, bf16[256,384]{1,0:T(8,128)(2,1)S(1)} %constant_dynamic-slice_fusion.1), kind=kOutput, calls=%fused_computation.15 | convolution fusion | flops 911278080 | bytes 5309952 | tf_op jit(solution)/shard_map/dot_general | solution.py:24
  54.0 1.7 fusion.11.col_ref
  55.7 1.8 fusion.8.row_ref
  57.5 23.1 %pair_forward.2 = (bf16[32768,1024]{1,0:T(8,128)(2,1)}, bf16[32768,128]{1,0:T(8,128)(2,1)}, bf16[16,128,2048]{2,1,0:T(8,128)(2,1)}, bf16[32768,128]{1,0:T(8,128)(2,1)}, bf16[16,128,2048]{2,1,0:T(8,128)(2,1)}) custom-call(bf16[256,128,128]{2,1,0:T(8,128)(2,1)} %pair_ref.3, f32[256,128]{1,0:T(8,128)} %fusion.8.row_ref, f32[128,128]{1,0:T(8,128)} %fusion.11.col_ref, ...), custom_call_target="tpu_custom_call" | custom-call | flops 5234491392 | bytes 40894464 | tf_op jit(solution)/shard_map/pair_forward/pallas_call | solution.py:299
  80.6 1.8 collective-permute-done.2
  82.6 9.5 %collective-permute-start.6 = (bf16[64,64,128]{2,1,0:T(8,128)(2,1)}, bf16[64,64,128]{2,1,0:T(8,128)(2,1)}, u32[]{:S(2)}, u32[]{:S(2)}) collective-permute-start(bf16[64,64,128]{2,1,0:T(8,128)(2,1)} %collective-permute-done), channel_id=1, source_target_pairs={{0,0},{1,1},{10,8},{11,9},{20,16},{21,17},{30,24},{31,25},{8,2},{9... | collective-permute-start | bytes 3145736 | tf_op jit(solution)/shard_map/ppermute | solution.py:330
  93.6 1.7 copy.49
  96.1 36.1 %pair_forward.3 = (bf16[32768,1024]{1,0:T(8,128)(2,1)}, bf16[32768,128]{1,0:T(8,128)(2,1)}, bf16[16,128,2048]{2,1,0:T(8,128)(2,1)}, bf16[32768,128]{1,0:T(8,128)(2,1)}, bf16[16,128,2048]{2,1,0:T(8,128)(2,1)}) custom-call(bf16[256,128,128]{2,1,0:T(8,128)(2,1)} %pair_ref.3, ...), custom_call_target="tpu_custom_call", output_to_operand_aliasing={{0}: (8, {}), {1}: (9, {}), {2}: (10, {}), {3}: (11, {}), {... | custom-call | flops 8724152320 | bytes 68157440 | tf_op jit(solution)/shard_map/pair_forward/pallas_call | solution.py:299
  132.2 2.8 collective-permute-start.4
  135.3 38.5 %pair_backward.2 = (bf16[256,128,128]{2,1,0:T(8,128)(2,1)}, f32[256,128]{1,0:T(8,128)}, f32[128,128]{1,0:T(8,128)}, f32[14,128,128]{2,1,0:T(8,128)}) custom-call(s32[1]{0:T(128)} %bitcast.idx_ref, bf16[256,128,128]{2,1,0:T(8,128)(2,1)} %cot_ref.3, s32[256,128]{1,0:T(8,128)} %mask_ref.3, bf16[64,64,128]{2,1,0:T(8,128)(2,1)} %collective-permute-done.6.refs_0_, ...), custom_call_target="tpu_custom_call" | custom-call | flops 14495514624 | bytes 60817408 | tf_op jit(solution)/shard_map/pair_backward/pallas_call | solution.py:369
  173.8 5.8 %collective-permute-done.5.refs_1_ = bf16[64,64,128]{2,1,0:T(8,128)(2,1)} collective-permute-done((bf16[64,64,128]{2,1,0:T(8,128)(2,1)}, bf16[64,64,128]{2,1,0:T(8,128)(2,1)}, u32[]{:S(2)}, u32[]{:S(2)}) %collective-permute-start.5) | collective-permute-done | bytes 1048608 | tf_op jit(solution)/shard_map/ppermute | solution.py:336
  179.6 38.6 %pair_backward.3 = (bf16[256,128,128]{2,1,0:T(8,128)(2,1)}, f32[256,128]{1,0:T(8,128)}, f32[128,128]{1,0:T(8,128)}, f32[14,128,128]{2,1,0:T(8,128)}) custom-call(s32[1]{0:T(128)} %bitcast.idx_ref, bf16[256,128,128]{2,1,0:T(8,128)(2,1)} %cot_ref.3, s32[256,128]{1,0:T(8,128)} %mask_ref.3, ...), custom_call_target="tpu_custom_call", output_to_operand_aliasing={{0}: (15, {}), {1}: (16, {})} | custom-call | flops 14495514624 | bytes 60817408 | tf_op jit(solution)/shard_map/pair_backward/pallas_call | solution.py:369
  218.2 0.9 convert_bitcast_fusion
  220.0 1.6 add_convert_fusion
  222.5 35.8 %all-to-all-start.1 = ((bf16[32,68,128]{2,1,0:T(8,128)(2,1)}), bf16[32,68,128]{2,1,0:T(8,128)(2,1)}, u32[]{:S(2)}, u32[]{:S(2)}) async-start(bf16[32,68,128]{2,1,0:T(8,128)(2,1)} %pad_maximum_fusion), calls=%async_computation.1 | async-start | bytes 1179648 | tf_op jit(solution)/shard_map/all_to_all | solution.py:416
  258.3 1.0 fusion.52
  259.6 4.5 %fusion.76 = f32[1024,1536]{1,0:T(8,128)} fusion(bf16[384,1536]{1,0:T(8,128)(2,1)S(1)} %copy-done, bf16[1024,384]{1,0:T(8,128)(2,1)S(1)} %bitcast.69, f32[1024]{0:T(1024)S(1)} %add_rsqrt_fusion), kind=kOutput, calls=%fused_computation.110 | convolution fusion | flops 1209139200 | bytes 8261632 | tf_op jit(solution)/shard_map/dot_general | solution.py:24
  264.1 11.8 %all-to-all-done.1 = bf16[32,68,128]{2,1,0:T(8,128)(2,1)} async-done(((bf16[32,68,128]{2,1,0:T(8,128)(2,1)}), bf16[32,68,128]{2,1,0:T(8,128)(2,1)}, u32[]{:S(2)}, u32[]{:S(2)}) %all-to-all-start.1) | async-done | bytes 557088 | tf_op jit(solution)/shard_map/all_to_all | solution.py:416
  275.9 1.1 convert_element_type.94
  277.1 1.0 copy-done.3
  279.0 0.9 broadcast_in_dim.22
  279.9 3.5 %all-to-all-start.2 = ((bf16[32,64,128]{2,1,0:T(8,128)(2,1)}), bf16[32,64,128]{2,1,0:T(8,128)(2,1)}, u32[]{:S(2)}, u32[]{:S(2)}) async-start(bf16[32,64,128]{2,1,0:T(8,128)(2,1)} %broadcast_in_dim.22), calls=%async_computation.2 | async-start | bytes 1048576 | tf_op jit(solution)/shard_map/all_to_all | solution.py:182
  283.4 7.6 %fusion.5 = bf16[1024,384]{1,0:T(8,128)(2,1)} fusion(bf16[1024,384]{1,0:T(8,128)(2,1)S(1)} %bitcast.70, bf16[1536,384]{1,0:T(8,128)(2,1)} %param.29, f32[1024,1536]{1,0:T(8,128)} %fusion.76, bf16[384,1536]{1,0:T(8,128)(2,1)S(1)} %copy-done.1, f32[1024]{0:T(1024)S(1)} %add_rsqrt_fusion), kind=kOutput, calls=%fused_computation.11 | convolution fusion | flops 2427715584 | bytes 10227712 | tf_op jit(solution)/shard_map/dot_general | solution.py:24
  291.0 1.2 fusion.32
  292.2 1.2 fusion.35
  294.1 5.4 %all-to-all-done.2 = bf16[32,64,128]{2,1,0:T(8,128)(2,1)} async-done(((bf16[32,64,128]{2,1,0:T(8,128)(2,1)}), bf16[32,64,128]{2,1,0:T(8,128)(2,1)}, u32[]{:S(2)}, u32[]{:S(2)}) %all-to-all-start.2) | async-done | bytes 524320 | tf_op jit(solution)/shard_map/all_to_all | solution.py:182
  299.4 1.1 fusion.78
  301.7 1.1 convolution_multiply_fusion.3
  302.8 1.1 convolution_multiply_fusion.2
  305.1 1.0 fusion.19
  307.3 1.1 fusion.30
  308.4 2.8 fusion.42
  311.2 1.6 broadcast_in_dim.23
  312.8 3.3 all-to-all-start.3
  316.1 1.6 fusion.46
  317.7 2.0 convolution_multiply_fusion.4
  319.7 1.0 convolution_multiply_fusion.5
  321.7 9.3 %all-to-all-done.3 = bf16[32,56,128]{2,1,0:T(8,128)(2,1)} async-done(((bf16[32,56,128]{2,1,0:T(8,128)(2,1)}), bf16[32,56,128]{2,1,0:T(8,128)(2,1)}, u32[]{:S(2)}, u32[]{:S(2)}) %all-to-all-start.3) | async-done | bytes 458784 | tf_op jit(solution)/shard_map/all_to_all | solution.py:182
  330.9 1.1 convert.26
  332.0 1.6 slice.61
  (98 shorter events, 19.7 us)
Async XLA Ops:
  0.6 46.9 %copy-start = (bf16[384,1536]{1,0:T(8,128)(2,1)S(1)}, bf16[384,1536]{1,0:T(8,128)(2,1)}, u32[]{:S(2)}) copy-start(bf16[384,1536]{1,0:T(8,128)(2,1)} %param.27) | copy-start | bytes 3538948
  2.4 43.4 %all-to-all-start = ((bf16[32,32,384]{2,1,0:T(8,128)(2,1)}), bf16[32,32,384]{2,1,0:T(8,128)(2,1)S(1)}, u32[]{:S(2)}, u32[]{:S(2)}) async-start(bf16[32,32,384]{2,1,0:T(8,128)(2,1)} %broadcast_in_dim.16), calls=%async_computation | async-start | bytes 1572864 | tf_op jit(solution)/shard_map/all_to_all | solution.py:182
  9.8 33.8 %copy-start.22 = (bf16[65,128]{1,0:T(8,128)(2,1)S(1)}, bf16[65,128]{1,0:T(8,128)(2,1)}, u32[]{:S(2)}) copy-start(bf16[65,128]{1,0:T(8,128)(2,1)} %param.24) | copy-start | bytes 49924
  9.8 34.4 %copy-start.13 = (bf16[128,512]{1,0:T(8,128)(2,1)S(1)}, bf16[128,512]{1,0:T(8,128)(2,1)}, u32[]{:S(2)}) copy-start(bf16[128,512]{1,0:T(8,128)(2,1)} %param.20) | copy-start | bytes 393220
  9.8 34.4 %copy-start.15 = (bf16[128,512]{1,0:T(8,128)(2,1)S(1)}, bf16[128,512]{1,0:T(8,128)(2,1)}, u32[]{:S(2)}) copy-start(bf16[128,512]{1,0:T(8,128)(2,1)} %param.21) | copy-start | bytes 393220
  22.0 58.6 %collective-permute-start = (bf16[64,64,128]{2,1,0:T(8,128)(2,1)}, bf16[64,64,128]{2,1,0:T(8,128)(2,1)}, u32[]{:S(2)}, u32[]{:S(2)}) collective-permute-start(bf16[64,64,128]{2,1,0:T(8,128)(2,1)} %get-tuple-element.52), channel_id=1, source_target_pairs={{0,0},{1,1},{2,10},{3,11},{4,20},{5,21},{6,30},{7,31},{8,8},{9,9},... | collective-permute-start | bytes 3145736 | tf_op jit(solution)/shard_map/ppermute | solution.py:263
  31.5 49.1 %collective-permute-start.1 = (bf16[64,64,128]{2,1,0:T(8,128)(2,1)}, bf16[64,64,128]{2,1,0:T(8,128)(2,1)}, u32[]{:S(2)}, u32[]{:S(2)}) collective-permute-start(bf16[64,64,128]{2,1,0:T(8,128)(2,1)} %get-tuple-element.53), channel_id=1, source_target_pairs={{0,8},{1,9},{2,18},{3,19},{4,28},{5,29},{6,6},{7,7},{8,16},{9,17},... | collective-permute-start | bytes 3145736 | tf_op jit(solution)/shard_map/ppermute | solution.py:263
  35.2 47.2 %collective-permute-start.2 = (bf16[64,64,128]{2,1,0:T(8,128)(2,1)}, bf16[64,64,128]{2,1,0:T(8,128)(2,1)}, u32[]{:S(2)}, u32[]{:S(2)}) collective-permute-start(bf16[64,64,128]{2,1,0:T(8,128)(2,1)} %get-tuple-element.54), channel_id=1, source_target_pairs={{0,16},{1,17},{2,26},{3,27},{4,4},{5,5},{6,14},{7,15},{8,24},{9,25... | collective-permute-start | bytes 3145736 | tf_op jit(solution)/shard_map/ppermute | solution.py:263
  38.6 44.0 %collective-permute-start.3 = (bf16[64,64,128]{2,1,0:T(8,128)(2,1)}, bf16[64,64,128]{2,1,0:T(8,128)(2,1)}, u32[]{:S(2)}, u32[]{:S(2)}) collective-permute-start(bf16[64,64,128]{2,1,0:T(8,128)(2,1)} %get-tuple-element.55), channel_id=1, source_target_pairs={{0,24},{1,25},{2,2},{3,3},{4,12},{5,13},{6,22},{7,23},{8,0},{9,1},... | collective-permute-start | bytes 3145736 | tf_op jit(solution)/shard_map/ppermute | solution.py:263
  47.6 2.2 copy-start.1
  49.8 4.2 %copy-start.16 = (bf16[384,128]{1,0:T(8,128)(2,1)S(1)}, bf16[384,128]{1,0:T(8,128)(2,1)}, u32[]{:S(2)}) copy-start(bf16[384,128]{1,0:T(8,128)(2,1)} %param.26) | copy-start | bytes 294916
  57.5 34.5 %copy-start.12 = (bf16[512,128]{1,0:T(8,128)(2,1)S(1)}, bf16[512,128]{1,0:T(8,128)(2,1)}, u32[]{:S(2)}) copy-start(bf16[512,128]{1,0:T(8,128)(2,1)} %down_ref.3) | copy-start | bytes 393220
  57.5 35.3 %copy-start.14 = (bf16[128,512]{1,0:T(8,128)(2,1)S(1)}, bf16[128,512]{1,0:T(8,128)(2,1)}, u32[]{:S(2)}) copy-start(bf16[128,512]{1,0:T(8,128)(2,1)} %param.20) | copy-start | bytes 393220
  57.5 37.7 %copy-start.21 = (bf16[128,128]{1,0:T(8,128)(2,1)S(1)}, bf16[128,128]{1,0:T(8,128)(2,1)}, u32[]{:S(2)}) copy-start(bf16[128,128]{1,0:T(8,128)(2,1)} %param.23) | copy-start | bytes 98308
  57.5 38.5 %copy-start.11 = (bf16[32,384]{1,0:T(8,128)(2,1)S(1)}, bf16[32,384]{1,0:T(8,128)(2,1)}, u32[]{:S(2)}) copy-start(bf16[32,384]{1,0:T(8,128)(2,1)} %param.18) | copy-start | bytes 73732
  82.6 52.7 %collective-permute-start.6 = (bf16[64,64,128]{2,1,0:T(8,128)(2,1)}, bf16[64,64,128]{2,1,0:T(8,128)(2,1)}, u32[]{:S(2)}, u32[]{:S(2)}) collective-permute-start(bf16[64,64,128]{2,1,0:T(8,128)(2,1)} %collective-permute-done), channel_id=1, source_target_pairs={{0,0},{1,1},{10,8},{11,9},{20,16},{21,17},{30,24},{31,25},{8,2},{9... | collective-permute-start | bytes 3145736 | tf_op jit(solution)/shard_map/ppermute | solution.py:330
  92.1 43.2 %collective-permute-start.7 = (bf16[64,64,128]{2,1,0:T(8,128)(2,1)}, bf16[64,64,128]{2,1,0:T(8,128)(2,1)}, u32[]{:S(2)}, u32[]{:S(2)}) collective-permute-start(bf16[64,64,128]{2,1,0:T(8,128)(2,1)} %collective-permute-done.2), channel_id=1, source_target_pairs={{16,1},{17,0},{26,9},{27,8},{4,17},{5,16},{14,25},{15,24},{24,3},{... | collective-permute-start | bytes 3145736 | tf_op jit(solution)/shard_map/ppermute | solution.py:330
  132.2 41.6 %collective-permute-start.4 = (bf16[64,64,128]{2,1,0:T(8,128)(2,1)}, bf16[64,64,128]{2,1,0:T(8,128)(2,1)}, u32[]{:S(2)}, u32[]{:S(2)}) collective-permute-start(bf16[64,64,128]{2,1,0:T(8,128)(2,1)} %collective-permute-done.1), channel_id=1, source_target_pairs={{8,0},{9,1},{18,8},{19,9},{28,16},{29,17},{6,24},{7,25},{16,2},{17... | collective-permute-start | bytes 3145736 | tf_op jit(solution)/shard_map/ppermute | solution.py:336
  135.0 44.6 %collective-permute-start.5 = (bf16[64,64,128]{2,1,0:T(8,128)(2,1)}, bf16[64,64,128]{2,1,0:T(8,128)(2,1)}, u32[]{:S(2)}, u32[]{:S(2)}) collective-permute-start(bf16[64,64,128]{2,1,0:T(8,128)(2,1)} %collective-permute-done.3), channel_id=1, source_target_pairs={{24,1},{25,0},{2,9},{3,8},{12,17},{13,16},{22,25},{23,24},{0,3},{1... | collective-permute-start | bytes 3145736 | tf_op jit(solution)/shard_map/ppermute | solution.py:336
  179.6 39.5 %copy-start.20 = (f32[128,128]{1,0:T(8,128)S(1)}, f32[128,128]{1,0:T(8,128)}, u32[]{:S(2)}) copy-start(f32[128,128]{1,0:T(8,128)} %get-tuple-element.86) | copy-start | bytes 196612
  222.5 53.4 %all-to-all-start.1 = ((bf16[32,68,128]{2,1,0:T(8,128)(2,1)}), bf16[32,68,128]{2,1,0:T(8,128)(2,1)}, u32[]{:S(2)}, u32[]{:S(2)}) async-start(bf16[32,68,128]{2,1,0:T(8,128)(2,1)} %pad_maximum_fusion), calls=%async_computation.1 | async-start | bytes 1179648 | tf_op jit(solution)/shard_map/all_to_all | solution.py:416
  277.0 1.0 copy-start.3
  279.9 19.5 %all-to-all-start.2 = ((bf16[32,64,128]{2,1,0:T(8,128)(2,1)}), bf16[32,64,128]{2,1,0:T(8,128)(2,1)}, u32[]{:S(2)}, u32[]{:S(2)}) async-start(bf16[32,64,128]{2,1,0:T(8,128)(2,1)} %broadcast_in_dim.22), calls=%async_computation.2 | async-start | bytes 1048576 | tf_op jit(solution)/shard_map/all_to_all | solution.py:182
  291.0 2.4 copy-start.4
  292.2 8.4 %copy-start.18 = (bf16[384,128]{1,0:T(8,128)(2,1)S(1)}, bf16[384,128]{1,0:T(8,128)(2,1)}, u32[]{:S(2)}) copy-start(bf16[384,128]{1,0:T(8,128)(2,1)} %param.25) | copy-start | bytes 294916
  300.6 1.1 copy-start.5
  301.1 2.8 copy-start.17
  303.9 1.3 copy-start.8
  305.1 2.2 copy-start.2
  305.1 2.2 copy-start.6
  306.6 0.7 copy-start.7
  312.8 18.1 %all-to-all-start.3 = ((bf16[32,56,128]{2,1,0:T(8,128)(2,1)}), bf16[32,56,128]{2,1,0:T(8,128)(2,1)}, u32[]{:S(2)}, u32[]{:S(2)}) async-start(bf16[32,56,128]{2,1,0:T(8,128)(2,1)} %broadcast_in_dim.23), calls=%async_computation.3 | async-start | bytes 917504 | tf_op jit(solution)/shard_map/all_to_all | solution.py:182
  316.1 3.6 %copy-start.9 = (f32[1024,48]{0,1:T(8,128)S(1)}, f32[1024,48]{0,1:T(8,128)}, u32[]{:S(2)}) copy-start(f32[1024,48]{0,1:T(8,128)} %fusion.32) | copy-start | bytes 589828
  316.1 3.6 %copy-start.10 = (f32[1024,48]{0,1:T(8,128)S(1)}, f32[1024,48]{0,1:T(8,128)}, u32[]{:S(2)}) copy-start(f32[1024,48]{0,1:T(8,128)} %fusion.35) | copy-start | bytes 589828
  316.1 3.6 %copy-start.19 = (f32[1024,48]{0,1:T(8,128)S(1)}, f32[1024,48]{0,1:T(8,128)}, u32[]{:S(2)}) copy-start(f32[1024,48]{0,1:T(8,128)} %fusion.19) | copy-start | bytes 589828
where the time goes:
time: 339 us; the launch traced here: 337 us
  Pallas kernels  148 us (44%)
  starting transfers between devices  82.4 us (24%)
  matrix products  37.7 us (11%)
  waiting for transfers between devices  34.2 us (10%)
  local copies, waits for them, and re-layouts  22.2 us (7%)
  other arithmetic  10.8 us (3%)
    pallas_call x2, Pallas kernels, local(): pl.pallas_call(functools.partial(backward_kernel, n_pieces, len(given)),...  77.1 us
    pallas_call x2, Pallas kernels, local(): pl.pallas_call(functools.partial(forward_kernel, span, len(saved)), grid=...  59.1 us
    all_to_all x1, starting transfers between devices, local(): lax.all_to_all(outgoing, axes, split_axis=0, concat_axis=0, tiled=True)  35.8 us
    dot_general x9, matrix products, product(): return jnp.dot(matrix_a, matrix_b, preferred_element_type=f32)  25.4 us
    ppermute x4, starting transfers between devices, local(): pieces[t] = lax.ppermute(sent[t], axes, spread)  19.9 us
    all_to_all x3, waiting for transfers between devices, gather_all(): return lax.all_to_all(copies, axes, split_axis=0, concat_axis=0, tiled=True)  14.6 us
    all_to_all x3, starting transfers between devices, gather_all(): return lax.all_to_all(copies, axes, split_axis=0, concat_axis=0, tiled=True)  14.2 us
    ppermute x4, starting transfers between devices, local(): pieces[t] = lax.ppermute(held[t], axes, onward(t))  12.5 us
  transfers between devices with their start and end apart: 12, of which 6 were waited for; matrix products, arithmetic and copies ran while one was open for 12% of the time, Pallas kernels for 33%

commit v1 on v0

--- a/solution.py
+++ b/solution.py
@@ -48,9 +48,8 @@
         @pl.when(pl.program_id(0) == turn)
         def _(turn=turn):
             for part in range(n_parts):
-                outs[turn * n_parts + part][...] = turned_ref[
-                    part * n_cols_piece:(part + 1) * n_cols_piece
-                ].astype(bf16)
+                start = (part + idx_ref[0]) % n_parts * n_cols_piece
+                outs[turn * n_parts + part][...] = turned_ref[pl.ds(start, n_cols_piece)].astype(bf16)
 
 
 def gates(both):
@@ -89,12 +88,13 @@
         out_t_ref[0, :, flat] = pair_out.T
 
 
-def backward_kernel(n_pieces, n_given, idx_ref, cot_ref, mask_ref, *refs):
+def backward_kernel(n_pieces, n_given, n_chained, idx_ref, cot_ref, mask_ref, *refs):
     mirror_refs = refs[:n_pieces]
     (both_ref, norm_ref, norm_t_ref, inv_ref, out_t_ref, bucket_ref,
      head_t_ref, down_t_ref, up_t_ref, gate_t_ref) = refs[n_pieces:n_pieces + 10]
-    refs = refs[n_pieces + 10 + n_given:]
-    grad_ref, rows_ref, cols_ref, sums_ref, mir_ref, ug_acc, down_acc, head_acc, rel_acc = refs
+    before = refs[n_pieces + 10 + n_given:n_pieces + 10 + n_given + n_chained]
+    refs = refs[n_pieces + 10 + n_given + n_chained:]
+    grad_ref, rows_ref, cols_ref, sums_ref, mir_ref, ug_acc, down_acc, head_acc, rel_acc, cols_acc = refs
     piece = pl.program_id(0)
     step = pl.program_id(1)
     first = (piece == 0) & (step == 0)
@@ -106,13 +106,21 @@
     hidden = down_t_ref.shape[1]
     bins = width // 2
 
+    n_slabs = hidden // lanes
+
     @pl.when(first)
     def _():
-        cols_ref[...] = jnp.zeros_like(cols_ref)
-        ug_acc[...] = jnp.zeros_like(ug_acc)
-        down_acc[...] = jnp.zeros_like(down_acc)
-        head_acc[...] = jnp.zeros_like(head_acc)
-        rel_acc[...] = jnp.zeros_like(rel_acc)
+        if before:
+            cols_acc[...] = before[0][...]
+            for q in range(2 * n_slabs):
+                ug_acc[:, q * lanes:(q + 1) * lanes] = before[1][q]
+            for q in range(n_slabs):
+                down_acc[:, q * lanes:(q + 1) * lanes] = before[1][2 * n_slabs + q].T
+            head_acc[...] = before[1][3 * n_slabs]
+            rel_acc[...] = before[1][3 * n_slabs + 1]
+        else:
+            for acc in (cols_acc, ug_acc, down_acc, head_acc, rel_acc):
+                acc[...] = jnp.zeros_like(acc)
 
     for t in range(n_pieces):
         @pl.when(piece == t)
@@ -145,8 +153,8 @@
         grad_tile = grad_in.reshape(n_rows, n_cols, width)
         grad_bf = grad_in.astype(bf16)
         grad_ref[rows] = grad_bf.reshape(n_rows, n_cols, width)
-        rows_ref[rows] = jnp.sum(grad_tile, axis=1)
-        cols_ref[...] += jnp.sum(grad_tile, axis=0)
+        rows_ref[rows] = jnp.sum(grad_tile, axis=1).astype(rows_ref.dtype)
+        cols_acc[...] += jnp.sum(grad_tile, axis=0)
         norm_t = norm_t_ref[0, :, flat]
         ug_acc[:, :hidden] += product(norm_t, grad_up)
         ug_acc[:, hidden:] += product(norm_t, grad_gate)
@@ -158,13 +166,22 @@
 
     @pl.when(last)
     def _():
-        n_slabs = hidden // lanes
-        for q in range(2 * n_slabs):
-            sums_ref[q] = ug_acc[:, q * lanes:(q + 1) * lanes]
-        for q in range(n_slabs):
-            sums_ref[2 * n_slabs + q] = down_acc[:, q * lanes:(q + 1) * lanes].T
-        sums_ref[3 * n_slabs] = head_acc[...]
-        sums_ref[3 * n_slabs + 1] = rel_acc[...]
+        cols_ref[...] = cols_acc[...].astype(cols_ref.dtype)
+        slabs = [ug_acc[:, q * lanes:(q + 1) * lanes] for q in range(2 * n_slabs)]
+        slabs += [down_acc[:, q * lanes:(q + 1) * lanes].T for q in range(n_slabs)]
+        for q, slab in enumerate(slabs + [head_acc[...], rel_acc[...]]):
+            sums_ref[q] = slab.astype(sums_ref.dtype)
+
+
+def unpack_kernel(slabs_ref, up_ref, gate_ref, down_ref, head_ref, rel_ref):
+    n_slabs = up_ref.shape[1] // lanes
+    for q in range(n_slabs):
+        at = slice(q * lanes, (q + 1) * lanes)
+        up_ref[:, at] = slabs_ref[q].astype(f32)
+        gate_ref[:, at] = slabs_ref[n_slabs + q].astype(f32)
+        down_ref[at] = slabs_ref[2 * n_slabs + q].astype(f32)
+    head_ref[...] = slabs_ref[3 * n_slabs].astype(f32)
+    rel_ref[...] = slabs_ref[3 * n_slabs + 1, :rel_ref.shape[0]].astype(f32)
 
 
 def transition(tokens_in, single_gate, single_up, single_down):
@@ -252,14 +269,17 @@
 
     every = [(r, k, b) for r in range(n_row) for k in range(n_row) for b in range(fold)]
 
-    def onward(t):
-        s = t // per_turn
-        return [(place((r + k + t) % n_row, k, b), place(k, r, (b + s) % fold)) for r, k, b in every]
+    def by_way(u, r, k, b):
+        return (r + k + u // per_turn * per_turn + (u % per_turn + b) % per_turn) % n_row
+
+    def onward(u):
+        s = u // per_turn
+        return [(place(by_way(u, r, k, b), k, b), place(k, r, (b + s) % fold)) for r, k, b in every]
 
     order = [t for group_no in range(n_groups) for t in range(group_no, n_row, n_groups)]
     pieces = {}
     for t in order:
-        spread = [(place(r, k, b), place((r + k + t) % n_row, k, b)) for r, k, b in every]
+        spread = [(place(r, k, b), place(by_way(t, r, k, b), k, b)) for r, k, b in every]
         pieces[t] = lax.ppermute(sent[t], axes, spread)
     singles = gather_all(single_repr, n_dev).reshape(tokens, -1)
 
@@ -292,8 +312,10 @@
     tile = lambda where: pl.BlockSpec((block_rows, tile_cols, width), lambda *at: (where(*at), 0, 0))
     some = lambda cols_, where: pl.BlockSpec((block_rows, cols_), lambda *at: (where(*at), 0))
     saved = ()
-    n_early = n_blocks * 3 // 8
-    for low, high in ((0, n_early), (n_early, n_blocks)):
+    held = pieces
+    pieces = {}
+    cuts = (0, n_blocks * 3 // 8, n_blocks * 13 // 16, n_blocks)
+    for low, high in zip(cuts[:-1], cuts[1:]):
         part = lambda i, low=low: i + low
         operands = [pair_repr, row_proj, col_proj, rpos, cpos, table, up_gate, pair_down]
         saved = pl.pallas_call(
@@ -323,17 +345,12 @@
             ),
             name="pair_forward",
         )(*operands, *saved)
-        if low == 0:
-            held, inv_held = lax.optimization_barrier((pieces, saved[3]))
+        number = cuts.index(low)
+        if number < 2:
+            held, inv_held = lax.optimization_barrier((held, saved[3]))
             saved = list(saved[:3]) + [inv_held] + list(saved[4:])
-            for t in range(0, n_row, n_groups):
+            for t in range(number, n_row, 2):
                 pieces[t] = lax.ppermute(held[t], axes, onward(t))
-    late = [t for t in range(n_row) if t % n_groups]
-    if late:
-        held, inv_held = lax.optimization_barrier((held, saved[3]))
-        saved = list(saved[:3]) + [inv_held] + list(saved[4:])
-        for t in late:
-            pieces[t] = lax.ppermute(held[t], axes, onward(t))
 
     head_t = head_weight.T
     down_t = pair_down.T
@@ -341,13 +358,12 @@
     gate_t = pair_gate.T
     steps = piece_rows // block_rows
     n_pieces = n_row // n_groups
-    given = ()
-    sums, cols = 0.0, 0.0
+    given, chained = (), ()
     for group_no in range(n_groups):
         def block_of(p, j, idx, group_no=group_no):
             t = p * n_groups + group_no
             strip_no = (idx[0] + fold - t // per_turn) % fold
-            return strip_no * (tile_cols // block_rows) + (t % per_turn) * steps + j
+            return strip_no * (tile_cols // block_rows) + (t % per_turn + strip_no) % per_turn * steps + j
 
         def mirror_map(p, j, idx, own=0):
             return (jnp.where(p == own, j, jnp.where(p < own, 0, steps - 1)), 0, 0)
@@ -362,12 +378,14 @@
                flat(width, block_of), lead((width, count), block_of), lead((1, count), block_of),
                whole(head_t.shape), whole(down_t.shape), whole(up_t.shape), whole(gate_t.shape)]
             + [pl.BlockSpec(memory_space=pl.ANY)] * len(given)
+            + [whole(x.shape) for x in chained]
         )
         operands = [logit_cotangent, pair_mask] + [pieces[p * n_groups + group_no] for p in range(n_pieces)] + list(saved) + [
-            bucket, head_t, down_t, up_t, gate_t] + list(given)
-        first_given = 1 + len(operands) - len(given)
-        pair_grad, row_part, col_part, sum_part = pl.pallas_call(
-            functools.partial(backward_kernel, n_pieces, len(given)),
+            bucket, head_t, down_t, up_t, gate_t] + list(given) + list(chained)
+        first_given = 1 + len(operands) - len(given) - len(chained)
+        kept = bf16 if group_no == n_groups - 1 else f32
+        pair_grad, row_part, cols, sums = pl.pallas_call(
+            functools.partial(backward_kernel, n_pieces, len(given), len(chained)),
             grid_spec=pltpu.PrefetchScalarGridSpec(
                 num_scalar_prefetch=1,
                 grid=(n_pieces, steps),
@@ -381,13 +399,14 @@
                     pltpu.VMEM((width, hidden), f32),
                     pltpu.VMEM((width, lanes), f32),
                     pltpu.VMEM((lanes, width), f32),
+                    pltpu.VMEM((tile_cols, width), f32),
                 ],
             ),
             out_shape=[
                 jax.ShapeDtypeStruct(pair_repr.shape, bf16),
-                jax.ShapeDtypeStruct((tile_rows, width), f32),
-                jax.ShapeDtypeStruct((tile_cols, width), f32),
-                jax.ShapeDtypeStruct((n_sums, lanes, lanes), f32),
+                jax.ShapeDtypeStruct((tile_rows, width), bf16),
+                jax.ShapeDtypeStruct((tile_cols, width), kept),
+                jax.ShapeDtypeStruct((n_sums, lanes, lanes), kept),
             ],
             input_output_aliases={first_given + i: i for i in range(len(given))},
             cost_estimate=pl.CostEstimate(
@@ -397,9 +416,7 @@
             ),
             name="pair_backward",
         )(core_arr, *operands)
-        given = (pair_grad, row_part)
-        sums = sums + sum_part
-        cols = cols + col_part
+        given, chained = (pair_grad, row_part), (cols, sums)
 
     sum_rows = n_sums * lanes // n_dev
 
@@ -410,7 +427,7 @@
 
     row_sent, col_sent = spread_out(row_part), spread_out(cols)
     row_len, col_len = row_sent.shape[1], col_sent.shape[1]
-    outgoing = jnp.concatenate([sums.reshape(n_dev, sum_rows, lanes), row_sent, col_sent], axis=1).astype(bf16)
+    outgoing = jnp.concatenate([sums.reshape(n_dev, sum_rows, lanes), row_sent, col_sent], axis=1)
     outgoing, singles = lax.optimization_barrier((outgoing, singles))
     s_normed_bf, _, updated = transition(singles, single_gate, single_up, single_down)
     arrived = lax.all_to_all(outgoing, axes, split_axis=0, concat_axis=0, tiled=True).astype(f32)
@@ -424,7 +441,7 @@
     totals_all = gather_all(totals, n_dev)
     own_sums, totals_all = lax.optimization_barrier((own_sums, totals_all))
     shared = gather_all(own_sums, n_dev)
-    slabs = shared.reshape(n_sums, lanes, lanes).astype(f32)
+    slabs = shared.reshape(n_sums, lanes, lanes)
 
     def tokens_of(held, n_strips, length):
         used = tokens * width // (n_strips * n_dev * length)
@@ -466,17 +483,21 @@
         my_grad_normed - my_normed * jnp.mean(my_grad_normed * my_normed, axis=-1, keepdims=True)
     )
 
-    def wide(first):
-        return slabs[first:first + n_slabs].transpose(1, 0, 2).reshape(width, hidden)
-
+    pair_sums = pl.pallas_call(
+        unpack_kernel,
+        out_shape=[
+            jax.ShapeDtypeStruct(pair_up.shape, f32),
+            jax.ShapeDtypeStruct(pair_gate.shape, f32),
+            jax.ShapeDtypeStruct(pair_down.shape, f32),
+            jax.ShapeDtypeStruct(head_weight.shape, f32),
+            jax.ShapeDtypeStruct(rel_table.shape, f32),
+        ],
+        name="unpack_sums",
+    )(slabs)
     return (
         pair_grad,
         single_grad.astype(bf16),
-        wide(0),
-        wide(n_slabs),
-        slabs[2 * n_slabs:3 * n_slabs].reshape(hidden, width),
-        slabs[3 * n_slabs],
-        slabs[3 * n_slabs + 1][:n_rel],
+        *pair_sums,
         prow_sum * grad_scale,
         pcol_sum * grad_scale,
         gate_sum * grad_scale,

time: 339 us -> 325 us (0.959)
  waiting for transfers between devices: 34.2 us -> 26.4 us
  Pallas kernels: 148 us -> 155 us
  starting transfers between devices: 82.4 us -> 77.6 us
  local copies, waits for them, and re-layouts: 22.2 us -> 17.4 us
    all_to_all x1, starting transfers between devices: 35.8 us -> 28.4 us  [local(): lax.all_to_all(outgoing, axes, split_axis=0, concat_axis=0, tiled=True)]
    ppermute x4, waiting for transfers between devices: 5.8 us -> 0.01 us  [local(): pieces[t] = lax.ppermute(held[t], axes, onward(t))]
    pallas_call x2 -> x3, Pallas kernels: 59.1 us -> 62.5 us  [local(): pl.pallas_call(functools.partial(forward_kernel, span, len(saved)), grid=...]
    pallas_call x2 -> x3, Pallas kernels: 77.1 us -> 79.9 us  [the longest x2 78 us: local(): pl.pallas_call(functools.partial(backward_kernel, n_pieces, len(given), l...]
    unnamed x52 -> x48, local copies, waits for them, and re-layouts: 8.74 us -> 7.06 us
  transfers between devices with their start and end apart: 12 -> 12, of which waited for: 6 -> 3; matrix products, arithmetic and copies ran while one was open for 12% -> 13% of each run, Pallas kernels for 33% -> 35%
where the time goes in v1:
time: 325 us; the launch traced here: 322 us
  Pallas kernels  155 us (48%)
  starting transfers between devices  77.6 us (24%)
  matrix products  37.7 us (12%)
  waiting for transfers between devices  26.4 us (8%)
  local copies, waits for them, and re-layouts  17.4 us (5%)
  other arithmetic  7.49 us (2%)
    pallas_call x2, Pallas kernels, local(): pl.pallas_call(functools.partial(backward_kernel, n_pieces, len(given), l...  78 us
    pallas_call x3, Pallas kernels, local(): pl.pallas_call(functools.partial(forward_kernel, span, len(saved)), grid=...  62.5 us
    all_to_all x1, starting transfers between devices, local(): lax.all_to_all(outgoing, axes, split_axis=0, concat_axis=0, tiled=True)  28.4 us
    dot_general x9, matrix products, product(): return jnp.dot(matrix_a, matrix_b, preferred_element_type=f32)  25.4 us
    ppermute x4, starting transfers between devices, local(): pieces[t] = lax.ppermute(sent[t], axes, spread)  19.9 us
    ppermute x4, starting transfers between devices, local(): pieces[t] = lax.ppermute(held[t], axes, onward(t))  15.3 us
    all_to_all x3, waiting for transfers between devices, gather_all(): return lax.all_to_all(copies, axes, split_axis=0, concat_axis=0, tiled=True)  14.8 us
    all_to_all x3, starting transfers between devices, gather_all(): return lax.all_to_all(copies, axes, split_axis=0, concat_axis=0, tiled=True)  14 us
  transfers between devices with their start and end apart: 12, of which 3 were waited for; matrix products, arithmetic and copies ran while one was open for 13% of the time, Pallas kernels for 35%

profile of v1, /device:TPU:0, one launch (start us, length us, event | category | flops | bytes accessed | tf_op | source)
XLA Modules:
  0.0 322.3 jit_solution(8857659740371245877)
XLA Ops:
  0.7 1.8 broadcast_in_dim.16
  2.4 7.3 %all-to-all-start = ((bf16[32,32,384]{2,1,0:T(8,128)(2,1)}), bf16[32,32,384]{2,1,0:T(8,128)(2,1)S(1)}, u32[]{:S(2)}, u32[]{:S(2)}) async-start(bf16[32,32,384]{2,1,0:T(8,128)(2,1)} %broadcast_in_dim.16), calls=%async_computation | async-start | bytes 1572864 | tf_op jit(solution)/shard_map/all_to_all | solution.py:199
  9.8 12.2 %mask_and_turn.1 = (bf16[64,64,128]{2,1,0:T(8,128)(2,1)}, bf16[64,64,128]{2,1,0:T(8,128)(2,1)}, bf16[64,64,128]{2,1,0:T(8,128)(2,1)}, bf16[64,64,128]{2,1,0:T(8,128)(2,1)}) custom-call(s32[1]{0:T(128)} %bitcast.idx_ref, bf16[2,2,64,128,128]{4,3,2,1,0:T(8,128)(2,1)} %bitcast.52, s32[2,2,64,128]{3,2,1,0:T(8,128)} %bitcast.66), custom_call_target="tpu_custom_call" | custom-call | flops 16777216 | bytes 12582912 | tf_op jit(solution)/shard_map/mask_and_turn/pallas_call | solution.py:244
  22.0 9.5 %collective-permute-start = (bf16[64,64,128]{2,1,0:T(8,128)(2,1)}, bf16[64,64,128]{2,1,0:T(8,128)(2,1)}, u32[]{:S(2)}, u32[]{:S(2)}) collective-permute-start(bf16[64,64,128]{2,1,0:T(8,128)(2,1)} %get-tuple-element.62), channel_id=1, source_target_pairs={{0,0},{1,9},{2,10},{3,19},{4,20},{5,29},{6,30},{7,7},{8,8},{9,17},... | collective-permute-start | bytes 3145736 | tf_op jit(solution)/shard_map/ppermute | solution.py:283
  31.5 3.7 %collective-permute-start.1 = (bf16[64,64,128]{2,1,0:T(8,128)(2,1)}, bf16[64,64,128]{2,1,0:T(8,128)(2,1)}, u32[]{:S(2)}, u32[]{:S(2)}) collective-permute-start(bf16[64,64,128]{2,1,0:T(8,128)(2,1)} %get-tuple-element.63), channel_id=1, source_target_pairs={{0,8},{1,1},{2,18},{3,11},{4,28},{5,21},{6,6},{7,31},{8,16},{9,9},... | collective-permute-start | bytes 3145736 | tf_op jit(solution)/shard_map/ppermute | solution.py:283
  35.2 3.4 %collective-permute-start.2 = (bf16[64,64,128]{2,1,0:T(8,128)(2,1)}, bf16[64,64,128]{2,1,0:T(8,128)(2,1)}, u32[]{:S(2)}, u32[]{:S(2)}) collective-permute-start(bf16[64,64,128]{2,1,0:T(8,128)(2,1)} %get-tuple-element.64), channel_id=1, source_target_pairs={{0,16},{1,25},{2,26},{3,3},{4,4},{5,13},{6,14},{7,23},{8,24},{9,1}... | collective-permute-start | bytes 3145736 | tf_op jit(solution)/shard_map/ppermute | solution.py:283
  38.6 3.4 %collective-permute-start.3 = (bf16[64,64,128]{2,1,0:T(8,128)(2,1)}, bf16[64,64,128]{2,1,0:T(8,128)(2,1)}, u32[]{:S(2)}, u32[]{:S(2)}) collective-permute-start(bf16[64,64,128]{2,1,0:T(8,128)(2,1)} %get-tuple-element.65), channel_id=1, source_target_pairs={{0,24},{1,17},{2,2},{3,27},{4,12},{5,5},{6,22},{7,15},{8,0},{9,25}... | collective-permute-start | bytes 3145736 | tf_op jit(solution)/shard_map/ppermute | solution.py:283
  45.0 0.9 clamp_add_fusion.refs_7_
  47.6 2.2 fusion.16
  49.8 4.2 %fusion.7 = bf16[384,384]{1,0:T(8,128)(2,1)} fusion(bf16[1536,384]{1,0:T(8,128)(2,1)} %param.29, bf16[384,1536]{1,0:T(8,128)(2,1)S(1)} %copy-done.1, f32[384,1536]{1,0:T(8,128)} %fusion.16, f32[384]{0:T(512)S(1)} %add_rsqrt_fusion.1, bf16[128,384]{1,0:T(8,128)(2,1)S(1)} %constant_dynamic-slice_fusion, bf16[256,384]{1,0:T(8,128)(2,1)S(1)} %constant_dynamic-slice_fusion.1), kind=kOutput, calls=%fused_computation.15 | convolution fusion | flops 911278080 | bytes 5309952 | tf_op jit(solution)/shard_map/dot_general | solution.py:24
  54.0 1.7 fusion.11.col_ref
  55.7 1.8 fusion.8.row_ref
  57.6 23.1 %pair_forward.3 = (bf16[32768,1024]{1,0:T(8,128)(2,1)}, bf16[32768,128]{1,0:T(8,128)(2,1)}, bf16[16,128,2048]{2,1,0:T(8,128)(2,1)}, bf16[32768,128]{1,0:T(8,128)(2,1)}, bf16[16,128,2048]{2,1,0:T(8,128)(2,1)}) custom-call(bf16[256,128,128]{2,1,0:T(8,128)(2,1)} %pair_ref.5, f32[256,128]{1,0:T(8,128)} %fusion.8.row_ref, f32[128,128]{1,0:T(8,128)} %fusion.11.col_ref, ...), custom_call_target="tpu_custom_call" | custom-call | flops 5234491392 | bytes 40894464 | tf_op jit(solution)/shard_map/pair_forward/pallas_call | solution.py:321
  80.7 9.5 %collective-permute-start.6 = (bf16[64,64,128]{2,1,0:T(8,128)(2,1)}, bf16[64,64,128]{2,1,0:T(8,128)(2,1)}, u32[]{:S(2)}, u32[]{:S(2)}) collective-permute-start(bf16[64,64,128]{2,1,0:T(8,128)(2,1)} %collective-permute-done), channel_id=1, source_target_pairs={{0,0},{9,1},{10,8},{19,9},{20,16},{29,17},{30,24},{7,25},{8,2},{17... | collective-permute-start | bytes 3145736 | tf_op jit(solution)/shard_map/ppermute | solution.py:353
  91.7 1.7 copy.50
  94.2 26.3 %pair_forward.4 = (bf16[32768,1024]{1,0:T(8,128)(2,1)}, bf16[32768,128]{1,0:T(8,128)(2,1)}, bf16[16,128,2048]{2,1,0:T(8,128)(2,1)}, bf16[32768,128]{1,0:T(8,128)(2,1)}, bf16[16,128,2048]{2,1,0:T(8,128)(2,1)}) custom-call(bf16[256,128,128]{2,1,0:T(8,128)(2,1)} %pair_ref.5, ...), custom_call_target="tpu_custom_call", output_to_operand_aliasing={{0}: (8, {}), {1}: (9, {}), {2}: (10, {}), {3}: (11, {}), {... | custom-call | flops 6106906624 | bytes 47710208 | tf_op jit(solution)/shard_map/pair_forward/pallas_call | solution.py:321
  120.5 5.6 %collective-permute-start.4 = (bf16[64,64,128]{2,1,0:T(8,128)(2,1)}, bf16[64,64,128]{2,1,0:T(8,128)(2,1)}, u32[]{:S(2)}, u32[]{:S(2)}) collective-permute-start(bf16[64,64,128]{2,1,0:T(8,128)(2,1)} %collective-permute-done.1), channel_id=1, source_target_pairs={{8,0},{1,1},{18,8},{11,9},{28,16},{21,17},{6,24},{31,25},{16,2},{9... | collective-permute-start | bytes 3145736 | tf_op jit(solution)/shard_map/ppermute | solution.py:353
  126.3 13.2 %pair_forward.5 = (bf16[32768,1024]{1,0:T(8,128)(2,1)}, bf16[32768,128]{1,0:T(8,128)(2,1)}, bf16[16,128,2048]{2,1,0:T(8,128)(2,1)}, bf16[32768,128]{1,0:T(8,128)(2,1)}, bf16[16,128,2048]{2,1,0:T(8,128)(2,1)}) custom-call(bf16[256,128,128]{2,1,0:T(8,128)(2,1)} %pair_ref.5, ...), custom_call_target="tpu_custom_call", output_to_operand_aliasing={{0}: (8, {}), {1}: (9, {}), {2}: (10, {}), {3}: (11, {}), {... | custom-call | flops 2617245696 | bytes 20447232 | tf_op jit(solution)/shard_map/pair_forward/pallas_call | solution.py:321
  139.5 38.9 %pair_backward.2 = (bf16[256,128,128]{2,1,0:T(8,128)(2,1)}, bf16[256,128]{1,0:T(8,128)(2,1)}, f32[128,128]{1,0:T(8,128)}, f32[14,128,128]{2,1,0:T(8,128)}) custom-call(s32[1]{0:T(128)} %bitcast.idx_ref, bf16[256,128,128]{2,1,0:T(8,128)(2,1)} %cot_ref.3, s32[256,128]{1,0:T(8,128)} %mask_ref.3, bf16[64,64,128]{2,1,0:T(8,128)(2,1)} %collective-permute-done.6.refs_0_, ...), custom_call_target="tpu_custom_call" | custom-call | flops 14495514624 | bytes 60817408 | tf_op jit(solution)/shard_map/pair_backward/pallas_call | solution.py:387
  178.4 39.1 %pair_backward.3 = (bf16[256,128,128]{2,1,0:T(8,128)(2,1)}, bf16[256,128]{1,0:T(8,128)(2,1)}, bf16[128,128]{1,0:T(8,128)(2,1)}, bf16[14,128,128]{2,1,0:T(8,128)(2,1)}) custom-call(s32[1]{0:T(128)} %bitcast.idx_ref, bf16[256,128,128]{2,1,0:T(8,128)(2,1)} %cot_ref.3, s32[256,128]{1,0:T(8,128)} %mask_ref.3, ...), custom_call_target="tpu_custom_call", output_to_operand_aliasing={{0}: (15, {}), {1}: (16, {})} | custom-call | flops 14495514624 | bytes 60817408 | tf_op jit(solution)/shard_map/pair_backward/pallas_call | solution.py:387
  217.5 2.0 pad_maximum_fusion
  219.5 28.4 %all-to-all-start.1 = ((bf16[32,68,128]{2,1,0:T(8,128)(2,1)}), bf16[32,68,128]{2,1,0:T(8,128)(2,1)}, u32[]{:S(2)}, u32[]{:S(2)}) async-start(bf16[32,68,128]{2,1,0:T(8,128)(2,1)} %pad_maximum_fusion), calls=%async_computation.1 | async-start | bytes 1179648 | tf_op jit(solution)/shard_map/all_to_all | solution.py:433
  247.9 1.0 fusion.52
  249.2 4.5 %fusion.76 = f32[1024,1536]{1,0:T(8,128)} fusion(bf16[384,1536]{1,0:T(8,128)(2,1)S(1)} %copy-done, bf16[1024,384]{1,0:T(8,128)(2,1)S(1)} %bitcast.56, f32[1024]{0:T(1024)S(1)} %add_rsqrt_fusion), kind=kOutput, calls=%fused_computation.103 | convolution fusion | flops 1209139200 | bytes 8261632 | tf_op jit(solution)/shard_map/dot_general | solution.py:24
  253.7 11.6 %all-to-all-done.1 = bf16[32,68,128]{2,1,0:T(8,128)(2,1)} async-done(((bf16[32,68,128]{2,1,0:T(8,128)(2,1)}), bf16[32,68,128]{2,1,0:T(8,128)(2,1)}, u32[]{:S(2)}, u32[]{:S(2)}) %all-to-all-start.1) | async-done | bytes 557088 | tf_op jit(solution)/shard_map/all_to_all | solution.py:433
  265.3 1.1 convert_element_type.87
  266.5 1.0 copy-done.3
  268.4 0.9 broadcast_in_dim.22
  269.3 3.3 %all-to-all-start.2 = ((bf16[32,64,128]{2,1,0:T(8,128)(2,1)}), bf16[32,64,128]{2,1,0:T(8,128)(2,1)}, u32[]{:S(2)}, u32[]{:S(2)}) async-start(bf16[32,64,128]{2,1,0:T(8,128)(2,1)} %broadcast_in_dim.22), calls=%async_computation.2 | async-start | bytes 1048576 | tf_op jit(solution)/shard_map/all_to_all | solution.py:199
  272.6 7.6 %fusion.5 = bf16[1024,384]{1,0:T(8,128)(2,1)} fusion(bf16[1024,384]{1,0:T(8,128)(2,1)S(1)} %bitcast.57, bf16[1536,384]{1,0:T(8,128)(2,1)} %param.29, f32[1024,1536]{1,0:T(8,128)} %fusion.76, bf16[384,1536]{1,0:T(8,128)(2,1)S(1)} %copy-done.1, f32[1024]{0:T(1024)S(1)} %add_rsqrt_fusion), kind=kOutput, calls=%fused_computation.11 | convolution fusion | flops 2427715584 | bytes 10227712 | tf_op jit(solution)/shard_map/dot_general | solution.py:24
  280.2 1.2 fusion.32
  281.4 1.2 fusion.35
  283.3 5.6 %all-to-all-done.2 = bf16[32,64,128]{2,1,0:T(8,128)(2,1)} async-done(((bf16[32,64,128]{2,1,0:T(8,128)(2,1)}), bf16[32,64,128]{2,1,0:T(8,128)(2,1)}, u32[]{:S(2)}, u32[]{:S(2)}) %all-to-all-start.2) | async-done | bytes 524320 | tf_op jit(solution)/shard_map/all_to_all | solution.py:199
  288.8 1.1 fusion.78
  291.1 1.1 convolution_multiply_fusion.3
  292.2 1.1 convolution_multiply_fusion.2
  293.7 0.9 copy-done.8
  294.6 1.0 fusion.19
  296.7 1.1 fusion.30
  297.9 2.8 fusion.42
  300.6 1.6 broadcast_in_dim.23
  302.2 3.3 %all-to-all-start.3 = ((bf16[32,56,128]{2,1,0:T(8,128)(2,1)}), bf16[32,56,128]{2,1,0:T(8,128)(2,1)}, u32[]{:S(2)}, u32[]{:S(2)}) async-start(bf16[32,56,128]{2,1,0:T(8,128)(2,1)} %broadcast_in_dim.23), calls=%async_computation.3 | async-start | bytes 917504 | tf_op jit(solution)/shard_map/all_to_all | solution.py:199
  305.5 1.6 fusion.46
  307.1 2.0 convolution_multiply_fusion.4
  309.1 1.0 convolution_multiply_fusion.5
  310.2 0.9 convolution_multiply_fusion.6
  311.1 9.3 %all-to-all-done.3 = bf16[32,56,128]{2,1,0:T(8,128)(2,1)} async-done(((bf16[32,56,128]{2,1,0:T(8,128)(2,1)}), bf16[32,56,128]{2,1,0:T(8,128)(2,1)}, u32[]{:S(2)}, u32[]{:S(2)}) %all-to-all-start.3) | async-done | bytes 458784 | tf_op jit(solution)/shard_map/all_to_all | solution.py:199
  320.3 1.9 unpack_sums.1
  (86 shorter events, 11.9 us)
Async XLA Ops:
  0.6 47.0 %copy-start = (bf16[384,1536]{1,0:T(8,128)(2,1)S(1)}, bf16[384,1536]{1,0:T(8,128)(2,1)}, u32[]{:S(2)}) copy-start(bf16[384,1536]{1,0:T(8,128)(2,1)} %param.27) | copy-start | bytes 3538948
  2.4 43.5 %all-to-all-start = ((bf16[32,32,384]{2,1,0:T(8,128)(2,1)}), bf16[32,32,384]{2,1,0:T(8,128)(2,1)S(1)}, u32[]{:S(2)}, u32[]{:S(2)}) async-start(bf16[32,32,384]{2,1,0:T(8,128)(2,1)} %broadcast_in_dim.16), calls=%async_computation | async-start | bytes 1572864 | tf_op jit(solution)/shard_map/all_to_all | solution.py:199
  9.8 33.8 %copy-start.21 = (bf16[65,128]{1,0:T(8,128)(2,1)S(1)}, bf16[65,128]{1,0:T(8,128)(2,1)}, u32[]{:S(2)}) copy-start(bf16[65,128]{1,0:T(8,128)(2,1)} %param.24) | copy-start | bytes 49924
  9.8 34.4 %copy-start.13 = (bf16[128,512]{1,0:T(8,128)(2,1)S(1)}, bf16[128,512]{1,0:T(8,128)(2,1)}, u32[]{:S(2)}) copy-start(bf16[128,512]{1,0:T(8,128)(2,1)} %param.20) | copy-start | bytes 393220
  9.8 34.4 %copy-start.15 = (bf16[128,512]{1,0:T(8,128)(2,1)S(1)}, bf16[128,512]{1,0:T(8,128)(2,1)}, u32[]{:S(2)}) copy-start(bf16[128,512]{1,0:T(8,128)(2,1)} %param.21) | copy-start | bytes 393220
  22.0 58.6 %collective-permute-start = (bf16[64,64,128]{2,1,0:T(8,128)(2,1)}, bf16[64,64,128]{2,1,0:T(8,128)(2,1)}, u32[]{:S(2)}, u32[]{:S(2)}) collective-permute-start(bf16[64,64,128]{2,1,0:T(8,128)(2,1)} %get-tuple-element.62), channel_id=1, source_target_pairs={{0,0},{1,9},{2,10},{3,19},{4,20},{5,29},{6,30},{7,7},{8,8},{9,17},... | collective-permute-start | bytes 3145736 | tf_op jit(solution)/shard_map/ppermute | solution.py:283
  31.5 49.1 %collective-permute-start.1 = (bf16[64,64,128]{2,1,0:T(8,128)(2,1)}, bf16[64,64,128]{2,1,0:T(8,128)(2,1)}, u32[]{:S(2)}, u32[]{:S(2)}) collective-permute-start(bf16[64,64,128]{2,1,0:T(8,128)(2,1)} %get-tuple-element.63), channel_id=1, source_target_pairs={{0,8},{1,1},{2,18},{3,11},{4,28},{5,21},{6,6},{7,31},{8,16},{9,9},... | collective-permute-start | bytes 3145736 | tf_op jit(solution)/shard_map/ppermute | solution.py:283
  35.2 45.4 %collective-permute-start.2 = (bf16[64,64,128]{2,1,0:T(8,128)(2,1)}, bf16[64,64,128]{2,1,0:T(8,128)(2,1)}, u32[]{:S(2)}, u32[]{:S(2)}) collective-permute-start(bf16[64,64,128]{2,1,0:T(8,128)(2,1)} %get-tuple-element.64), channel_id=1, source_target_pairs={{0,16},{1,25},{2,26},{3,3},{4,4},{5,13},{6,14},{7,23},{8,24},{9,1}... | collective-permute-start | bytes 3145736 | tf_op jit(solution)/shard_map/ppermute | solution.py:283
  38.6 42.1 %collective-permute-start.3 = (bf16[64,64,128]{2,1,0:T(8,128)(2,1)}, bf16[64,64,128]{2,1,0:T(8,128)(2,1)}, u32[]{:S(2)}, u32[]{:S(2)}) collective-permute-start(bf16[64,64,128]{2,1,0:T(8,128)(2,1)} %get-tuple-element.65), channel_id=1, source_target_pairs={{0,24},{1,17},{2,2},{3,27},{4,12},{5,5},{6,22},{7,15},{8,0},{9,25}... | collective-permute-start | bytes 3145736 | tf_op jit(solution)/shard_map/ppermute | solution.py:283
  47.6 2.2 copy-start.1
  49.8 4.2 %copy-start.16 = (bf16[384,128]{1,0:T(8,128)(2,1)S(1)}, bf16[384,128]{1,0:T(8,128)(2,1)}, u32[]{:S(2)}) copy-start(bf16[384,128]{1,0:T(8,128)(2,1)} %param.26) | copy-start | bytes 294916
  57.6 32.6 %copy-start.9 = (bf16[512,128]{1,0:T(8,128)(2,1)S(1)}, bf16[512,128]{1,0:T(8,128)(2,1)}, u32[]{:S(2)}) copy-start(bf16[512,128]{1,0:T(8,128)(2,1)} %down_ref.5) | copy-start | bytes 393220
  57.6 33.4 %copy-start.14 = (bf16[128,512]{1,0:T(8,128)(2,1)S(1)}, bf16[128,512]{1,0:T(8,128)(2,1)}, u32[]{:S(2)}) copy-start(bf16[128,512]{1,0:T(8,128)(2,1)} %param.20) | copy-start | bytes 393220
  57.6 35.8 %copy-start.20 = (bf16[128,128]{1,0:T(8,128)(2,1)S(1)}, bf16[128,128]{1,0:T(8,128)(2,1)}, u32[]{:S(2)}) copy-start(bf16[128,128]{1,0:T(8,128)(2,1)} %param.23) | copy-start | bytes 98308
  57.6 36.5 %copy-start.12 = (bf16[32,384]{1,0:T(8,128)(2,1)S(1)}, bf16[32,384]{1,0:T(8,128)(2,1)}, u32[]{:S(2)}) copy-start(bf16[32,384]{1,0:T(8,128)(2,1)} %param.18) | copy-start | bytes 73732
  80.7 58.8 %collective-permute-start.6 = (bf16[64,64,128]{2,1,0:T(8,128)(2,1)}, bf16[64,64,128]{2,1,0:T(8,128)(2,1)}, u32[]{:S(2)}, u32[]{:S(2)}) collective-permute-start(bf16[64,64,128]{2,1,0:T(8,128)(2,1)} %collective-permute-done), channel_id=1, source_target_pairs={{0,0},{9,1},{10,8},{19,9},{20,16},{29,17},{30,24},{7,25},{8,2},{17... | collective-permute-start | bytes 3145736 | tf_op jit(solution)/shard_map/ppermute | solution.py:353
  90.1 49.3 %collective-permute-start.7 = (bf16[64,64,128]{2,1,0:T(8,128)(2,1)}, bf16[64,64,128]{2,1,0:T(8,128)(2,1)}, u32[]{:S(2)}, u32[]{:S(2)}) collective-permute-start(bf16[64,64,128]{2,1,0:T(8,128)(2,1)} %collective-permute-done.2), channel_id=1, source_target_pairs={{16,1},{25,0},{26,9},{3,8},{4,17},{13,16},{14,25},{23,24},{24,3},{... | collective-permute-start | bytes 3145736 | tf_op jit(solution)/shard_map/ppermute | solution.py:353
  120.5 57.9 %collective-permute-start.4 = (bf16[64,64,128]{2,1,0:T(8,128)(2,1)}, bf16[64,64,128]{2,1,0:T(8,128)(2,1)}, u32[]{:S(2)}, u32[]{:S(2)}) collective-permute-start(bf16[64,64,128]{2,1,0:T(8,128)(2,1)} %collective-permute-done.1), channel_id=1, source_target_pairs={{8,0},{1,1},{18,8},{11,9},{28,16},{21,17},{6,24},{31,25},{16,2},{9... | collective-permute-start | bytes 3145736 | tf_op jit(solution)/shard_map/ppermute | solution.py:353
  126.0 52.3 %collective-permute-start.5 = (bf16[64,64,128]{2,1,0:T(8,128)(2,1)}, bf16[64,64,128]{2,1,0:T(8,128)(2,1)}, u32[]{:S(2)}, u32[]{:S(2)}) collective-permute-start(bf16[64,64,128]{2,1,0:T(8,128)(2,1)} %collective-permute-done.3), channel_id=1, source_target_pairs={{24,1},{17,0},{2,9},{27,8},{12,17},{5,16},{22,25},{15,24},{0,3},{2... | collective-permute-start | bytes 3145736 | tf_op jit(solution)/shard_map/ppermute | solution.py:353
  219.5 45.8 %all-to-all-start.1 = ((bf16[32,68,128]{2,1,0:T(8,128)(2,1)}), bf16[32,68,128]{2,1,0:T(8,128)(2,1)}, u32[]{:S(2)}, u32[]{:S(2)}) async-start(bf16[32,68,128]{2,1,0:T(8,128)(2,1)} %pad_maximum_fusion), calls=%async_computation.1 | async-start | bytes 1179648 | tf_op jit(solution)/shard_map/all_to_all | solution.py:433
  266.5 1.0 copy-start.3
  269.3 19.5 %all-to-all-start.2 = ((bf16[32,64,128]{2,1,0:T(8,128)(2,1)}), bf16[32,64,128]{2,1,0:T(8,128)(2,1)}, u32[]{:S(2)}, u32[]{:S(2)}) async-start(bf16[32,64,128]{2,1,0:T(8,128)(2,1)} %broadcast_in_dim.22), calls=%async_computation.2 | async-start | bytes 1048576 | tf_op jit(solution)/shard_map/all_to_all | solution.py:199
  280.2 2.4 copy-start.4
  281.4 8.6 %copy-start.18 = (bf16[384,128]{1,0:T(8,128)(2,1)S(1)}, bf16[384,128]{1,0:T(8,128)(2,1)}, u32[]{:S(2)}) copy-start(bf16[384,128]{1,0:T(8,128)(2,1)} %param.25) | copy-start | bytes 294916
  290.0 1.1 copy-start.5
  290.5 2.8 copy-start.17
  293.3 1.3 copy-start.8
  294.6 2.2 copy-start.2
  294.6 2.2 copy-start.6
  296.0 0.7 copy-start.7
  302.2 18.1 %all-to-all-start.3 = ((bf16[32,56,128]{2,1,0:T(8,128)(2,1)}), bf16[32,56,128]{2,1,0:T(8,128)(2,1)}, u32[]{:S(2)}, u32[]{:S(2)}) async-start(bf16[32,56,128]{2,1,0:T(8,128)(2,1)} %broadcast_in_dim.23), calls=%async_computation.3 | async-start | bytes 917504 | tf_op jit(solution)/shard_map/all_to_all | solution.py:199
  305.5 3.6 %copy-start.10 = (f32[1024,48]{0,1:T(8,128)S(1)}, f32[1024,48]{0,1:T(8,128)}, u32[]{:S(2)}) copy-start(f32[1024,48]{0,1:T(8,128)} %fusion.32) | copy-start | bytes 589828
  305.5 3.6 %copy-start.11 = (f32[1024,48]{0,1:T(8,128)S(1)}, f32[1024,48]{0,1:T(8,128)}, u32[]{:S(2)}) copy-start(f32[1024,48]{0,1:T(8,128)} %fusion.35) | copy-start | bytes 589828
  305.5 3.6 %copy-start.19 = (f32[1024,48]{0,1:T(8,128)S(1)}, f32[1024,48]{0,1:T(8,128)}, u32[]{:S(2)}) copy-start(f32[1024,48]{0,1:T(8,128)} %fusion.19) | copy-start | bytes 589828
